TPU v7x, 512 devices: a whole 4x8x8 slice. The times are simulated.
512 devices in a mesh: dp: 8 (over y_lo, core), ctx: 64 (over x, y_hi, z).
Axes of the slice: x: 4, y: 8 (y_hi: 2, y_lo: 4; y = y_hi * 4 + y_lo), z: 8, core: 2. Of those that a mesh axis runs over, the one named last changes fastest.
Arguments:
- tokens: bfloat16 [8, 32768, 1024], P('dp', 'ctx'), may hold values from -6 to 6
- w_query: bfloat16 [1024, 1024], P('dp')
- w_key: bfloat16 [1024, 1024], P('dp')
- w_value: bfloat16 [1024, 1024], P('dp'), may hold values from -0.1875 to 0.1875
- w_output: bfloat16 [1024, 1024], P('dp'), may hold values from -0.1875 to 0.1875
- nbr_index: int32 [8, 256, 8], P('dp', 'ctx'), may hold values from 0 to 255, as said below
- nbr_count: int32 [8, 256], P('dp', 'ctx'), may hold values from 1 to 8, as said below
Outputs:
- update: bfloat16 [8, 32768, 1024], P('dp', 'ctx')
Inputs may be any that keep to these rules, and one draw needn't show every extreme that they name: `nbr_index`: in each row the first nbr_count slots name distinct blocks, slot 0 names the query block itself, and every slot names a block at most 8 blocks away from it; unused slots name blocks of that same range. In every draw some block is exactly 8 away from a query block that uses it. `nbr_count`: in every draw some query block uses all 8 slots.
All inputs are finite; a program needn't handle non-finite values.
Results may differ from a plain program's by a relative error of at most 0.0089.
Values may be sent and summed in bfloat16 or wider, within the bound.
No kernel may reach another device: no remote copies, remote signals or barrier semaphores. Data moves between devices by JAX's collectives and lax.ppermute only.
A program may use at most 128 MiB of HBM per device.

v0:
```python
import jax
import jax.numpy as jnp
from jax import lax
from jax.sharding import PartitionSpec as P

HEADS = 8
HD = 128
BLK = 128
MAXN = 8
REACH = 2


def from_behind(value, axis, steps):
    count = lax.axis_size(axis)
    leading, last = (max(0, -steps), min(count, count - steps))
    return lax.ppermute(value, axis, [(source, source + steps) for source in range(leading, last)])


def attend_block(query_blk, key_sel, value_sel, used):
    query_heads = query_blk.reshape(BLK, HEADS, HD)
    key_heads = key_sel.reshape(MAXN * BLK, HEADS, HD)
    value_heads = value_sel.reshape(MAXN * BLK, HEADS, HD)
    scores = jnp.einsum(
        "qhd,khd->hqk", query_heads, key_heads, preferred_element_type=jnp.float32
    ) * HD ** (-0.5)
    slot_used = jnp.arange(MAXN * BLK) // BLK < used
    scores = jnp.where(slot_used[None, None, :], scores, -1e30)
    peak = jnp.max(scores, axis=-1, keepdims=True)
    expo = jnp.exp(scores - peak) * slot_used[None, None, :].astype(jnp.float32)
    weights = (expo / jnp.sum(expo, axis=-1, keepdims=True)).astype(jnp.bfloat16)
    attended = jnp.einsum("hqk,khd->qhd", weights, value_heads, preferred_element_type=jnp.float32)
    return attended.reshape(BLK, HEADS * HD).astype(jnp.bfloat16)


def move_far(payload, offset):
    return from_behind((payload[0], payload[1]), "ctx", offset)


def collect_window(payload):
    lower = []
    upper = []
    for offset in list(range(REACH, 0, -1)) + list(range(-1, -REACH - 1, -1)):
        moved = move_far(payload, offset)
        if offset > 0:
            lower.append(moved)
        else:
            upper.append(moved)
    return (lower, upper)


def project_pair(rows_in, full_key, full_value):
    keys = jnp.dot(rows_in, full_key, preferred_element_type=jnp.float32).astype(jnp.bfloat16)
    values = jnp.dot(rows_in, full_value, preferred_element_type=jnp.float32).astype(jnp.bfloat16)
    return (keys, values)


def gather_window(keys, values):
    lower, upper = collect_window((keys, values))
    pieces = lower + [(keys, values)] + upper
    key_window = jnp.concatenate([item[0] for item in pieces], axis=0)
    value_window = jnp.concatenate([item[1] for item in pieces], axis=0)
    return (key_window, value_window)


def body(tokens, w_query, w_key, w_value, w_output, nbr_index, nbr_count):
    local_tok = tokens[0]
    blocks = local_tok.shape[0] // BLK
    rank = lax.axis_index("ctx")
    values_f = local_tok.astype(jnp.float32)
    normed = (
        values_f * lax.rsqrt(jnp.mean(values_f * values_f, axis=-1, keepdims=True) + 1e-05)
    ).astype(jnp.bfloat16)
    full_query, full_key, full_value, full_output = (
        lax.all_gather(w_query, "dp", axis=0, tiled=True),
        lax.all_gather(w_key, "dp", axis=0, tiled=True),
        lax.all_gather(w_value, "dp", axis=0, tiled=True),
        lax.all_gather(w_output, "dp", axis=0, tiled=True),
    )
    keys, values = project_pair(normed, full_key, full_value)
    key_window, value_window = gather_window(keys, values)
    queries = jnp.dot(normed, full_query, preferred_element_type=jnp.float32).astype(jnp.bfloat16)
    width = HEADS * HD
    key_blocks = key_window.reshape(-1, BLK, width)
    value_blocks = value_window.reshape(-1, BLK, width)
    first_block = rank * blocks - REACH * blocks
    local_index = nbr_index[0] - first_block
    query_blocks = queries.reshape(blocks, BLK, width)

    def per_block(items):
        query_blk, index_row, used = items
        key_sel = jnp.take(key_blocks, index_row, axis=0)
        value_sel = jnp.take(value_blocks, index_row, axis=0)
        return attend_block(query_blk, key_sel, value_sel, used)

    attended = lax.map(per_block, (query_blocks, local_index, nbr_count[0])).reshape(
        blocks * BLK, width
    )
    update = jnp.dot(attended, full_output, preferred_element_type=jnp.float32).astype(jnp.bfloat16)
    return update[None]


def solution(mesh):
    placed = (
        P("dp", "ctx", None),
        P("dp", None),
        P("dp", None),
        P("dp", None),
        P("dp", None),
        P("dp", "ctx", None),
        P("dp", "ctx"),
    )
    return jax.shard_map(
        body, mesh=mesh, in_specs=placed, out_specs=P("dp", "ctx", None), check_vma=False
    )
```

profile of v0, /device:TPU:59, one launch (start us, length us, event | category | flops | bytes accessed | tf_op | source)
XLA Modules:
  0.0 534.2 jit_solution(2425077717888437057)
XLA Ops:
  10.3 45.3 %all-gather.9.cloned.1.call-done = bf16[1024,1024]{1,0:T(8,128)(2,1)} async-done(((bf16[128,1024]{1,0:T(8,128)(2,1)}), bf16[1024,1024]{1,0:T(8,128)(2,1)}) %all-gather.9.cloned.1.call-update) | async-done | bytes 2097168 | tf_op jit(solution)/shard_map/all_gather | solution.py:75
  55.6 3.2 convolution_convert_fusion.1
  58.8 4.3 collective-permute-start.4
  63.2 3.3 collective-permute-start.5
  66.5 33.6 %all-gather.5.cloned.1.call-done = bf16[1024,1024]{1,0:T(8,128)(2,1)} async-done(((bf16[128,1024]{1,0:T(8,128)(2,1)}), bf16[1024,1024]{1,0:T(8,128)(2,1)}) %all-gather.5.cloned.1.call-update) | async-done | bytes 2097168 | tf_op jit(solution)/shard_map/all_gather | solution.py:76
  100.0 2.9 convolution_convert_fusion.3
  102.9 3.4 collective-permute-start
  106.4 3.3 collective-permute-start.1
  109.7 76.0 %collective-permute-start.6 = (bf16[512,1024]{1,0:T(8,128)(2,1)S(1)}, bf16[512,1024]{1,0:T(8,128)(2,1)}, u32[]{:S(2)}, u32[]{:S(2)}) collective-permute-start(bf16[512,1024]{1,0:T(8,128)(2,1)S(1)} %convolution_convert_fusion.1), channel_id=1, source_target_pairs={{1,0},{2,1},{3,2},{4,3},{5,4},{6,5},{7,6},{8,7},{9,8},{10,9},{11,1... | collective-permute-start | bytes 3145736 | tf_op jit(solution)/shard_map/ppermute | solution.py:16
  185.7 4.3 collective-permute-start.7
  190.0 59.2 %all-gather.7.cloned.1.call-done = bf16[1024,1024]{1,0:T(8,128)(2,1)} async-done(((bf16[128,1024]{1,0:T(8,128)(2,1)}), bf16[1024,1024]{1,0:T(8,128)(2,1)}) %all-gather.7.cloned.1.call-update) | async-done | bytes 2097168 | tf_op jit(solution)/shard_map/all_gather | solution.py:74
  249.1 3.9 convolution_convert_fusion.2
  253.0 62.1 %collective-permute-start.2 = (bf16[512,1024]{1,0:T(8,128)(2,1)S(1)}, bf16[512,1024]{1,0:T(8,128)(2,1)S(1)}, u32[]{:S(2)}, u32[]{:S(2)}) collective-permute-start(bf16[512,1024]{1,0:T(8,128)(2,1)S(1)} %convolution_convert_fusion.3), channel_id=1, source_target_pairs={{1,0},{2,1},{3,2},{4,3},{5,4},{6,5},{7,6},{8,7},{9,8},{10,9},{11,1... | collective-permute-start | bytes 3145736 | tf_op jit(solution)/shard_map/ppermute | solution.py:16
  316.4 1.9 collective-permute-start.3
  325.0 97.5 %collective-permute-done.2 = bf16[512,1024]{1,0:T(8,128)(2,1)S(1)} collective-permute-done((bf16[512,1024]{1,0:T(8,128)(2,1)S(1)}, bf16[512,1024]{1,0:T(8,128)(2,1)S(1)}, u32[]{:S(2)}, u32[]{:S(2)}) %collective-permute-start.2) | collective-permute-done | bytes 1048608 | tf_op jit(solution)/shard_map/ppermute | solution.py:16
  422.6 21.2 %collective-permute-done.3 = bf16[512,1024]{1,0:T(8,128)(2,1)S(1)} collective-permute-done((bf16[512,1024]{1,0:T(8,128)(2,1)S(1)}, bf16[512,1024]{1,0:T(8,128)(2,1)S(1)}, u32[]{:S(2)}, u32[]{:S(2)}) %collective-permute-start.3) | collective-permute-done | bytes 1048608 | tf_op jit(solution)/shard_map/ppermute | solution.py:16
  443.9 2.3 copy-done.2
  446.2 77.2 %while.12 = (s32[]{:T(128)}, bf16[4,128,1024]{2,1,0:T(8,128)(2,1)}, s32[4,8]{1,0:T(4,128)S(1)}, bf16[20,128,1024]{2,1,0:T(8,128)(2,1)}, s32[4]{0:T(128)S(1)}, /*...) while((s32[]{:T(128)}, bf16[4,128,1024]{2,1,0:T(8,128)(2,1)}, ...), condition=%wide.region_4.6_spmd, body=%wide.region_1.5_spmd.sunk | while | flops 548548672 | bytes 57170744 | solution.py:95
  446.3 3.2 gather_fusion
  449.4 4.5 gather_fusion.1
  453.9 3.4 broadcast_select_fusion.3
  461.1 1.7 fusion.45
  465.6 3.2 gather_fusion
  468.7 4.5 gather_fusion.1
  473.2 3.4 broadcast_select_fusion.3
  484.9 3.2 gather_fusion
  488.1 4.5 gather_fusion.1
  492.6 3.4 broadcast_select_fusion.3
  504.2 3.2 gather_fusion
  507.4 4.5 gather_fusion.1
  511.9 3.4 broadcast_select_fusion.3
  523.5 4.1 fusion.22
  (97 shorter events, 43.0 us)
Async XLA Ops:
  6.5 49.1 %all-gather.9.cloned.1.call-start = ((), (), s32[]{:S(2)}) async-start(), calls=%async_computation.2 | async-start | bytes 2359296 | tf_op jit(solution)/shard_map/all_gather | solution.py:75
  7.3 92.8 %all-gather.5.cloned.1.call-start = ((), (), s32[]{:S(2)}) async-start(), calls=%async_computation | async-start | bytes 2359296 | tf_op jit(solution)/shard_map/all_gather | solution.py:76
  8.0 241.1 %all-gather.7.cloned.1.call-start = ((), (), s32[]{:S(2)}) async-start(), calls=%async_computation.1 | async-start | bytes 2359296 | tf_op jit(solution)/shard_map/all_gather | solution.py:74
  8.7 514.8 %all-gather.11.cloned.1.call-start = ((), (), s32[]{:S(2)}) async-start(), calls=%async_computation.3 | async-start | bytes 2359296 | tf_op jit(solution)/shard_map/all_gather | solution.py:77
  10.3 89.7 %copy-start.3 = (bf16[1,512,1024]{2,1,0:T(8,128)(2,1)S(1)}, bf16[1,512,1024]{2,1,0:T(8,128)(2,1)}, u32[]{:S(2)}) copy-start(bf16[1,512,1024]{2,1,0:T(8,128)(2,1)} %param.11) | copy-start | bytes 3145732
  58.8 50.9 %copy-start.4 = (s32[1,4,8]{2,1,0:T(4,128)S(1)}, s32[1,4,8]{2,1,0:T(4,128)}, u32[]{:S(2)}) copy-start(s32[1,4,8]{2,1,0:T(4,128)} %param.16) | copy-start | bytes 388
  58.8 126.9 %collective-permute-start.4 = (bf16[512,1024]{1,0:T(8,128)(2,1)S(1)}, bf16[512,1024]{1,0:T(8,128)(2,1)}, u32[]{:S(2)}, u32[]{:S(2)}) collective-permute-start(bf16[512,1024]{1,0:T(8,128)(2,1)S(1)} %convolution_convert_fusion.1), channel_id=1, source_target_pairs={{0,2},{1,3},{2,4},{3,5},{4,6},{5,7},{6,8},{7,9},{8,10},{9,11},{10,... | collective-permute-start | bytes 3145736 | tf_op jit(solution)/shard_map/ppermute | solution.py:16
  63.2 189.8 %collective-permute-start.5 = (bf16[512,1024]{1,0:T(8,128)(2,1)S(1)}, bf16[512,1024]{1,0:T(8,128)(2,1)}, u32[]{:S(2)}, u32[]{:S(2)}) collective-permute-start(bf16[512,1024]{1,0:T(8,128)(2,1)S(1)} %convolution_convert_fusion.1), channel_id=1, source_target_pairs={{0,1},{1,2},{2,3},{3,4},{4,5},{5,6},{6,7},{7,8},{8,9},{9,10},{10,1... | collective-permute-start | bytes 3145736 | tf_op jit(solution)/shard_map/ppermute | solution.py:16
  102.9 213.5 %collective-permute-start = (bf16[512,1024]{1,0:T(8,128)(2,1)S(1)}, bf16[512,1024]{1,0:T(8,128)(2,1)}, u32[]{:S(2)}, u32[]{:S(2)}) collective-permute-start(bf16[512,1024]{1,0:T(8,128)(2,1)S(1)} %convolution_convert_fusion.3), channel_id=1, source_target_pairs={{0,2},{1,3},{2,4},{3,5},{4,6},{5,7},{6,8},{7,9},{8,10},{9,11},{10,... | collective-permute-start | bytes 3145736 | tf_op jit(solution)/shard_map/ppermute | solution.py:16
  106.4 214.6 %collective-permute-start.1 = (bf16[512,1024]{1,0:T(8,128)(2,1)S(1)}, bf16[512,1024]{1,0:T(8,128)(2,1)}, u32[]{:S(2)}, u32[]{:S(2)}) collective-permute-start(bf16[512,1024]{1,0:T(8,128)(2,1)S(1)} %convolution_convert_fusion.3), channel_id=1, source_target_pairs={{0,1},{1,2},{2,3},{3,4},{4,5},{5,6},{6,7},{7,8},{8,9},{9,10},{10,1... | collective-permute-start | bytes 3145736 | tf_op jit(solution)/shard_map/ppermute | solution.py:16
  109.7 212.7 %collective-permute-start.6 = (bf16[512,1024]{1,0:T(8,128)(2,1)S(1)}, bf16[512,1024]{1,0:T(8,128)(2,1)}, u32[]{:S(2)}, u32[]{:S(2)}) collective-permute-start(bf16[512,1024]{1,0:T(8,128)(2,1)S(1)} %convolution_convert_fusion.1), channel_id=1, source_target_pairs={{1,0},{2,1},{3,2},{4,3},{5,4},{6,5},{7,6},{8,7},{9,8},{10,9},{11,1... | collective-permute-start | bytes 3145736 | tf_op jit(solution)/shard_map/ppermute | solution.py:16
  185.7 138.0 %collective-permute-start.7 = (bf16[512,1024]{1,0:T(8,128)(2,1)S(1)}, bf16[512,1024]{1,0:T(8,128)(2,1)}, u32[]{:S(2)}, u32[]{:S(2)}) collective-permute-start(bf16[512,1024]{1,0:T(8,128)(2,1)S(1)} %convolution_convert_fusion.1), channel_id=1, source_target_pairs={{2,0},{3,1},{4,2},{5,3},{6,4},{7,5},{8,6},{9,7},{10,8},{11,9},{12,... | collective-permute-start | bytes 3145736 | tf_op jit(solution)/shard_map/ppermute | solution.py:16
  253.0 169.6 %collective-permute-start.2 = (bf16[512,1024]{1,0:T(8,128)(2,1)S(1)}, bf16[512,1024]{1,0:T(8,128)(2,1)S(1)}, u32[]{:S(2)}, u32[]{:S(2)}) collective-permute-start(bf16[512,1024]{1,0:T(8,128)(2,1)S(1)} %convolution_convert_fusion.3), channel_id=1, source_target_pairs={{1,0},{2,1},{3,2},{4,3},{5,4},{6,5},{7,6},{8,7},{9,8},{10,9},{11,1... | collective-permute-start | bytes 3145736 | tf_op jit(solution)/shard_map/ppermute | solution.py:16
  316.4 127.4 %collective-permute-start.3 = (bf16[512,1024]{1,0:T(8,128)(2,1)S(1)}, bf16[512,1024]{1,0:T(8,128)(2,1)S(1)}, u32[]{:S(2)}, u32[]{:S(2)}) collective-permute-start(bf16[512,1024]{1,0:T(8,128)(2,1)S(1)} %convolution_convert_fusion.3), channel_id=1, source_target_pairs={{2,0},{3,1},{4,2},{5,3},{6,4},{7,5},{8,6},{9,7},{10,8},{11,9},{12,... | collective-permute-start | bytes 3145736 | tf_op jit(solution)/shard_map/ppermute | solution.py:16
  325.0 118.9 %copy-start.1 = (bf16[2560,1024]{1,0:T(8,128)(2,1)}, bf16[2560,1024]{1,0:T(8,128)(2,1)S(1)}, u32[]{:S(2)}) copy-start(bf16[2560,1024]{1,0:T(8,128)(2,1)S(1)} %constant_dynamic-update-slice_fusion.6) | copy-start | bytes 15728644
  325.0 121.2 %copy-start.5 = (s32[1,4]{1,0:T(1,128)S(1)}, s32[1,4]{1,0:T(1,128)}, u32[]{:S(2)}) copy-start(s32[1,4]{1,0:T(1,128)} %param.17) | copy-start | bytes 52
  443.9 2.3 copy-start.2
  461.1 1.7 copy-start
  480.4 1.7 copy-start
  499.7 1.7 copy-start
  519.0 1.7 copy-start
Sparse Core Ops, SparseCore 0:
  9.4 46.1 all-gather.8
  57.7 42.3 all-gather.4
  102.1 146.9 all-gather.6
  251.1 170.1 all-gather.10
where the time goes:
time: 535 us; the launch traced here: 534 us
  waiting for transfers between devices  259 us (48%)
  starting transfers between devices  159 us (30%)
  local copies, waits for them, and re-layouts  56.4 us (11%)
  other arithmetic  24.2 us (5%)
  matrix products  22.3 us (4%)
  between operations  13.4 us (3%)
    ppermute x8, starting transfers between devices, from_behind(): lax.ppermute(value, axis, [(source, source + steps) for source in range(l...  159 us
    ppermute x8, waiting for transfers between devices, from_behind(): lax.ppermute(value, axis, [(source, source + steps) for source in range(l...  119 us
    all_gather x1, waiting for transfers between devices, body(): lax.all_gather(w_query, 'dp', axis=0, tiled=True)  59.2 us
    all_gather x1, waiting for transfers between devices, body(): lax.all_gather(w_key, 'dp', axis=0, tiled=True)  45.3 us
    all_gather x1, waiting for transfers between devices, body(): lax.all_gather(w_value, 'dp', axis=0, tiled=True)  33.6 us
    gather x4, local copies, waits for them, and re-layouts, per_block(): key_sel = jnp.take(key_blocks, index_row, axis=0)  18 us
    select_n x4, other arithmetic, per_block(): value_sel = jnp.take(value_blocks, index_row, axis=0)  13.4 us
    gather x4, local copies, waits for them, and re-layouts, per_block(): value_sel = jnp.take(value_blocks, index_row, axis=0)  12.7 us
  transfers between devices with their start and end apart: 12, of which 5 were waited for; matrix products, arithmetic and copies ran while one was open for 18% of the time, Pallas kernels for 0%

commit v1 on v0

--- a/solution.py
+++ b/solution.py
@@ -8,6 +8,11 @@
 BLK = 128
 MAXN = 8
 REACH = 2
+
+
+def all_by_exchange(array, mesh_axis, dim):
+    repeated = jnp.stack([array] * lax.axis_size(mesh_axis))
+    return jnp.concatenate(lax.all_to_all(repeated, mesh_axis, 0, 0), axis=dim)
 
 
 def from_behind(value, axis, steps):
@@ -73,7 +78,7 @@
     full_query, full_key, full_value, full_output = (
         lax.all_gather(w_query, "dp", axis=0, tiled=True),
         lax.all_gather(w_key, "dp", axis=0, tiled=True),
-        lax.all_gather(w_value, "dp", axis=0, tiled=True),
+        all_by_exchange(w_value, "dp", 0),
         lax.all_gather(w_output, "dp", axis=0, tiled=True),
     )
     keys, values = project_pair(normed, full_key, full_value)

time: 535 us -> 552 us (1.032)
  the two profiles are of different devices: /device:TPU:59 before, /device:TPU:44 now
where the time goes in v1:
time: 552 us; the launch traced here: 551 us
  waiting for transfers between devices  330 us (60%)
  starting transfers between devices  102 us (18%)
  local copies, waits for them, and re-layouts  58.9 us (11%)
  other arithmetic  23.1 us (4%)
  matrix products  22.4 us (4%)
  between operations  13.3 us (2%)
    ppermute x8, waiting for transfers between devices, from_behind(): lax.ppermute(value, axis, [(source, source + steps) for source in range(l...  263 us
    ppermute x8, starting transfers between devices, from_behind(): lax.ppermute(value, axis, [(source, source + steps) for source in range(l...  97 us
    all_gather x1, waiting for transfers between devices, body(): lax.all_gather(w_key, 'dp', axis=0, tiled=True)  66.2 us
    gather x4, local copies, waits for them, and re-layouts, per_block(): key_sel = jnp.take(key_blocks, index_row, axis=0)  18 us
    select_n x4, other arithmetic, per_block(): value_sel = jnp.take(value_blocks, index_row, axis=0)  13.5 us
    gather x4, local copies, waits for them, and re-layouts, per_block(): value_sel = jnp.take(value_blocks, index_row, axis=0)  12.7 us
  transfers between devices with their start and end apart: 12, of which 5 were waited for; matrix products, arithmetic and copies ran while one was open for 18% of the time, Pallas kernels for 0%

profile of v1, /device:TPU:44, one launch (start us, length us, event | category | flops | bytes accessed | tf_op | source)
XLA Modules:
  0.0 550.6 jit_solution(10894884629813526581)
XLA Ops:
  7.3 2.5 stack.2
  9.8 5.0 all-to-all-start
  15.9 66.2 %all-gather.6.cloned.1.call-done = bf16[1024,1024]{1,0:T(8,128)(2,1)} async-done(((bf16[128,1024]{1,0:T(8,128)(2,1)}), bf16[1024,1024]{1,0:T(8,128)(2,1)}) %all-gather.6.cloned.1.call-update) | async-done | bytes 2097168 | tf_op jit(solution)/shard_map/all_gather | solution.py:80
  82.0 3.9 convolution_convert_fusion.1
  85.9 5.9 %collective-permute-start.4 = (bf16[512,1024]{1,0:T(8,128)(2,1)}, bf16[512,1024]{1,0:T(8,128)(2,1)}, u32[]{:S(2)}, u32[]{:S(2)}) collective-permute-start(bf16[512,1024]{1,0:T(8,128)(2,1)} %convolution_convert_fusion.1), channel_id=1, source_target_pairs={{0,2},{1,3},{2,4},{3,5},{4,6},{5,7},{6,8},{7,9},{8,10},{9,11},{10,... | collective-permute-start | bytes 3145736 | tf_op jit(solution)/shard_map/ppermute | solution.py:21
  91.9 4.1 collective-permute-start.5
  96.0 2.3 convolution_convert_fusion.3
  98.3 5.8 %collective-permute-start = (bf16[512,1024]{1,0:T(8,128)(2,1)}, bf16[512,1024]{1,0:T(8,128)(2,1)S(1)}, u32[]{:S(2)}, u32[]{:S(2)}) collective-permute-start(bf16[512,1024]{1,0:T(8,128)(2,1)} %convolution_convert_fusion.3), channel_id=1, source_target_pairs={{0,2},{1,3},{2,4},{3,5},{4,6},{5,7},{6,8},{7,9},{8,10},{9,11},{10,... | collective-permute-start | bytes 3145736 | tf_op jit(solution)/shard_map/ppermute | solution.py:21
  104.1 3.0 collective-permute-start.1
  107.2 8.8 %collective-permute-start.6 = (bf16[512,1024]{1,0:T(8,128)(2,1)}, bf16[512,1024]{1,0:T(8,128)(2,1)S(1)}, u32[]{:S(2)}, u32[]{:S(2)}) collective-permute-start(bf16[512,1024]{1,0:T(8,128)(2,1)} %convolution_convert_fusion.1), channel_id=1, source_target_pairs={{1,0},{2,1},{3,2},{4,3},{5,4},{6,5},{7,6},{8,7},{9,8},{10,9},{11,1... | collective-permute-start | bytes 3145736 | tf_op jit(solution)/shard_map/ppermute | solution.py:21
  116.0 100.6 %collective-permute-done.4 = bf16[512,1024]{1,0:T(8,128)(2,1)} collective-permute-done((bf16[512,1024]{1,0:T(8,128)(2,1)}, bf16[512,1024]{1,0:T(8,128)(2,1)}, u32[]{:S(2)}, u32[]{:S(2)}) %collective-permute-start.4) | collective-permute-done | bytes 1048608 | tf_op jit(solution)/shard_map/ppermute | solution.py:21
  218.6 3.9 convolution_convert_fusion.2
  222.5 63.5 %collective-permute-done.5 = bf16[512,1024]{1,0:T(8,128)(2,1)} collective-permute-done((bf16[512,1024]{1,0:T(8,128)(2,1)}, bf16[512,1024]{1,0:T(8,128)(2,1)}, u32[]{:S(2)}, u32[]{:S(2)}) %collective-permute-start.5) | collective-permute-done | bytes 1048608 | tf_op jit(solution)/shard_map/ppermute | solution.py:21
  286.0 65.5 %collective-permute-start.2 = (bf16[512,1024]{1,0:T(8,128)(2,1)}, bf16[512,1024]{1,0:T(8,128)(2,1)S(1)}, u32[]{:S(2)}, u32[]{:S(2)}) collective-permute-start(bf16[512,1024]{1,0:T(8,128)(2,1)} %convolution_convert_fusion.3), channel_id=1, source_target_pairs={{1,0},{2,1},{3,2},{4,3},{5,4},{6,5},{7,6},{8,7},{9,8},{10,9},{11,1... | collective-permute-start | bytes 3145736 | tf_op jit(solution)/shard_map/ppermute | solution.py:21
  352.8 1.9 collective-permute-start.3
  361.4 78.6 %collective-permute-done.2 = bf16[512,1024]{1,0:T(8,128)(2,1)S(1)} collective-permute-done((bf16[512,1024]{1,0:T(8,128)(2,1)}, bf16[512,1024]{1,0:T(8,128)(2,1)S(1)}, u32[]{:S(2)}, u32[]{:S(2)}) %collective-permute-start.2) | collective-permute-done | bytes 1048608 | tf_op jit(solution)/shard_map/ppermute | solution.py:21
  440.0 20.1 %collective-permute-done.3 = bf16[512,1024]{1,0:T(8,128)(2,1)S(1)} collective-permute-done((bf16[512,1024]{1,0:T(8,128)(2,1)}, bf16[512,1024]{1,0:T(8,128)(2,1)S(1)}, u32[]{:S(2)}, u32[]{:S(2)}) %collective-permute-start.3) | collective-permute-done | bytes 1048608 | tf_op jit(solution)/shard_map/ppermute | solution.py:21
  460.2 2.3 copy-done.2
  462.5 77.4 %while.12 = (s32[]{:T(128)}, bf16[4,128,1024]{2,1,0:T(8,128)(2,1)}, s32[4,8]{1,0:T(4,128)S(1)}, bf16[20,128,1024]{2,1,0:T(8,128)(2,1)}, s32[4]{0:T(128)S(1)}, /*...) while((s32[]{:T(128)}, bf16[4,128,1024]{2,1,0:T(8,128)(2,1)}, ...), condition=%wide.region_4.6_spmd, body=%wide.region_1.5_spmd.sunk | while | flops 548548672 | bytes 57170744 | solution.py:100
  462.5 3.2 gather_fusion
  465.7 4.5 gather_fusion.1
  470.2 3.4 broadcast_select_fusion.3
  481.9 3.2 gather_fusion
  485.0 4.5 gather_fusion.1
  489.5 3.4 broadcast_select_fusion.3
  501.2 3.2 gather_fusion
  504.4 4.5 gather_fusion.1
  508.9 3.4 broadcast_select_fusion.3
  520.6 3.2 gather_fusion
  523.8 4.5 gather_fusion.1
  528.3 3.4 broadcast_select_fusion.3
  539.9 4.1 fusion.25
  (97 shorter events, 44.7 us)
Async XLA Ops:
  6.5 75.5 %all-gather.6.cloned.1.call-start = ((), (), s32[]{:S(2)}) async-start(), calls=%async_computation.2 | async-start | bytes 2359296 | tf_op jit(solution)/shard_map/all_gather | solution.py:80
  9.8 5.8 %copy-start.3 = (bf16[1,512,1024]{2,1,0:T(8,128)(2,1)S(1)}, bf16[1,512,1024]{2,1,0:T(8,128)(2,1)}, u32[]{:S(2)}) copy-start(bf16[1,512,1024]{2,1,0:T(8,128)(2,1)} %param.11) | copy-start | bytes 3145732
  9.8 86.2 %all-to-all-start = ((bf16[8,128,1024]{2,1,0:T(8,128)(2,1)}), bf16[8,128,1024]{2,1,0:T(8,128)(2,1)S(1)}, u32[]{:S(2)}, u32[]{:S(2)}) async-start(bf16[8,128,1024]{2,1,0:T(8,128)(2,1)} %stack.2), calls=%async_computation | async-start | bytes 4194304 | tf_op jit(solution)/shard_map/all_to_all | solution.py:15
  14.8 203.8 %all-gather.4.cloned.1.call-start = ((), (), s32[]{:S(2)}) async-start(), calls=%async_computation.1 | async-start | bytes 2359296 | tf_op jit(solution)/shard_map/all_gather | solution.py:79
  15.5 524.4 %all-gather.8.cloned.1.call-start = ((), (), s32[]{:S(2)}) async-start(), calls=%async_computation.3 | async-start | bytes 2359296 | tf_op jit(solution)/shard_map/all_gather | solution.py:82
  85.9 130.7 %collective-permute-start.4 = (bf16[512,1024]{1,0:T(8,128)(2,1)}, bf16[512,1024]{1,0:T(8,128)(2,1)}, u32[]{:S(2)}, u32[]{:S(2)}) collective-permute-start(bf16[512,1024]{1,0:T(8,128)(2,1)} %convolution_convert_fusion.1), channel_id=1, source_target_pairs={{0,2},{1,3},{2,4},{3,5},{4,6},{5,7},{6,8},{7,9},{8,10},{9,11},{10,... | collective-permute-start | bytes 3145736 | tf_op jit(solution)/shard_map/ppermute | solution.py:21
  91.9 194.1 %collective-permute-start.5 = (bf16[512,1024]{1,0:T(8,128)(2,1)}, bf16[512,1024]{1,0:T(8,128)(2,1)}, u32[]{:S(2)}, u32[]{:S(2)}) collective-permute-start(bf16[512,1024]{1,0:T(8,128)(2,1)} %convolution_convert_fusion.1), channel_id=1, source_target_pairs={{0,1},{1,2},{2,3},{3,4},{4,5},{5,6},{6,7},{7,8},{8,9},{9,10},{10,1... | collective-permute-start | bytes 3145736 | tf_op jit(solution)/shard_map/ppermute | solution.py:21
  96.0 11.2 %copy-start.4 = (s32[1,4,8]{2,1,0:T(4,128)S(1)}, s32[1,4,8]{2,1,0:T(4,128)}, u32[]{:S(2)}) copy-start(s32[1,4,8]{2,1,0:T(4,128)} %param.16) | copy-start | bytes 388
  98.3 254.5 %collective-permute-start = (bf16[512,1024]{1,0:T(8,128)(2,1)}, bf16[512,1024]{1,0:T(8,128)(2,1)S(1)}, u32[]{:S(2)}, u32[]{:S(2)}) collective-permute-start(bf16[512,1024]{1,0:T(8,128)(2,1)} %convolution_convert_fusion.3), channel_id=1, source_target_pairs={{0,2},{1,3},{2,4},{3,5},{4,6},{5,7},{6,8},{7,9},{8,10},{9,11},{10,... | collective-permute-start | bytes 3145736 | tf_op jit(solution)/shard_map/ppermute | solution.py:21
  104.1 253.2 %collective-permute-start.1 = (bf16[512,1024]{1,0:T(8,128)(2,1)}, bf16[512,1024]{1,0:T(8,128)(2,1)}, u32[]{:S(2)}, u32[]{:S(2)}) collective-permute-start(bf16[512,1024]{1,0:T(8,128)(2,1)} %convolution_convert_fusion.3), channel_id=1, source_target_pairs={{0,1},{1,2},{2,3},{3,4},{4,5},{5,6},{6,7},{7,8},{8,9},{9,10},{10,1... | collective-permute-start | bytes 3145736 | tf_op jit(solution)/shard_map/ppermute | solution.py:21
  107.2 252.7 %collective-permute-start.6 = (bf16[512,1024]{1,0:T(8,128)(2,1)}, bf16[512,1024]{1,0:T(8,128)(2,1)S(1)}, u32[]{:S(2)}, u32[]{:S(2)}) collective-permute-start(bf16[512,1024]{1,0:T(8,128)(2,1)} %convolution_convert_fusion.1), channel_id=1, source_target_pairs={{1,0},{2,1},{3,2},{4,3},{5,4},{6,5},{7,6},{8,7},{9,8},{10,9},{11,1... | collective-permute-start | bytes 3145736 | tf_op jit(solution)/shard_map/ppermute | solution.py:21
  216.7 143.4 %collective-permute-start.7 = (bf16[512,1024]{1,0:T(8,128)(2,1)}, bf16[512,1024]{1,0:T(8,128)(2,1)}, u32[]{:S(2)}, u32[]{:S(2)}) collective-permute-start(bf16[512,1024]{1,0:T(8,128)(2,1)} %convolution_convert_fusion.1), channel_id=1, source_target_pairs={{2,0},{3,1},{4,2},{5,3},{6,4},{7,5},{8,6},{9,7},{10,8},{11,9},{12,... | collective-permute-start | bytes 3145736 | tf_op jit(solution)/shard_map/ppermute | solution.py:21
  286.0 154.0 %collective-permute-start.2 = (bf16[512,1024]{1,0:T(8,128)(2,1)}, bf16[512,1024]{1,0:T(8,128)(2,1)S(1)}, u32[]{:S(2)}, u32[]{:S(2)}) collective-permute-start(bf16[512,1024]{1,0:T(8,128)(2,1)} %convolution_convert_fusion.3), channel_id=1, source_target_pairs={{1,0},{2,1},{3,2},{4,3},{5,4},{6,5},{7,6},{8,7},{9,8},{10,9},{11,1... | collective-permute-start | bytes 3145736 | tf_op jit(solution)/shard_map/ppermute | solution.py:21
  352.8 107.4 %collective-permute-start.3 = (bf16[512,1024]{1,0:T(8,128)(2,1)}, bf16[512,1024]{1,0:T(8,128)(2,1)S(1)}, u32[]{:S(2)}, u32[]{:S(2)}) collective-permute-start(bf16[512,1024]{1,0:T(8,128)(2,1)} %convolution_convert_fusion.3), channel_id=1, source_target_pairs={{2,0},{3,1},{4,2},{5,3},{6,4},{7,5},{8,6},{9,7},{10,8},{11,9},{12,... | collective-permute-start | bytes 3145736 | tf_op jit(solution)/shard_map/ppermute | solution.py:21
  361.4 98.8 %copy-start.1 = (bf16[2560,1024]{1,0:T(8,128)(2,1)}, bf16[2560,1024]{1,0:T(8,128)(2,1)S(1)}, u32[]{:S(2)}) copy-start(bf16[2560,1024]{1,0:T(8,128)(2,1)S(1)} %constant_dynamic-update-slice_fusion.6) | copy-start | bytes 15728644
  361.4 101.1 %copy-start.5 = (s32[1,4]{1,0:T(1,128)S(1)}, s32[1,4]{1,0:T(1,128)}, u32[]{:S(2)}) copy-start(s32[1,4]{1,0:T(1,128)} %param.17) | copy-start | bytes 52
  460.2 2.3 copy-start.2
  477.4 1.7 copy-start
  496.7 1.7 copy-start
  516.1 1.7 copy-start
  535.4 1.7 copy-start
Sparse Core Ops, SparseCore 0:
  9.4 72.5 all-gather.5
  84.1 79.0 all-gather.3
  165.3 273.4 all-gather.7
